TPU v7x, 512 devices: a whole 4x8x8 slice. The times are simulated.
512 devices in a mesh: shard: 128 (over y, z, core), tensor: 4 (over x).
Axes of the slice: x: 4, y: 8, z: 8, core: 2. Of those that a mesh axis runs over, the one named last changes fastest.
Arguments:
- grad_query: bfloat16 [128, 1024, 512], P('shard', None, 'tensor'), may hold values from -8 to 8
- error_query: float32 [128, 1024, 512], P('shard', None, 'tensor'), may hold values from -3 to 3
- grad_output: bfloat16 [128, 512, 1024], P('shard', 'tensor'), may hold values from -8 to 8
- error_output: float32 [128, 512, 1024], P('shard', 'tensor'), may hold values from -3 to 3
- start_query: float32 [512, 32], P('tensor'), may hold values from -6 to 6
- start_output: float32 [1024, 32], replicated, may hold values from -6 to 6
- weight_query: float32 [1024, 512], P('shard', 'tensor'), may hold values from -0.1875 to 0.1875
- weight_output: float32 [512, 1024], P('tensor', 'shard'), may hold values from -0.25 to 0.25
- moment_query: float32 [1024, 512], P('shard', 'tensor'), may hold values from -1.2 to 1.2
- moment_output: float32 [512, 1024], P('tensor', 'shard'), may hold values from -1.2 to 1.2
- grad_vector: bfloat16 [128, 3584], P('shard'), may hold values from -12 to 12
- moment_vector: float32 [3584], P('shard'), may hold values from -1.2 to 1.2
- weight_vector: float32 [3584], P('shard'), may hold values from 0.5 to 1.5
Outputs:
- new_error_query: float32 [128, 1024, 512], P('shard', None, 'tensor')
- new_error_output: float32 [128, 512, 1024], P('shard', 'tensor')
- new_moment_query: float32 [1024, 512], P('shard', 'tensor')
- new_moment_output: float32 [512, 1024], P('tensor', 'shard')
- new_weight_query: float32 [1024, 512], P(None, 'tensor')
- new_weight_output: float32 [512, 1024], P('tensor')
- new_moment_vector: float32 [3584], P('shard')
- new_weight_vector: float32 [3584], replicated
All inputs are finite; a program needn't handle non-finite values.
Results may differ from a plain program's by a relative error of at most 0.0003.
Values sent between devices are 32-bit elements; how exact they have to be, the bound alone decides.
No kernel may reach another device: no remote copies, remote signals or barrier semaphores. Data moves between devices by JAX's collectives and lax.ppermute only.
A program may use at most 64 MiB of HBM per device.

v0:
```python
import jax
import jax.numpy as jnp
from jax import lax
from jax.sharding import PartitionSpec as P

ROUNDS = 2
highest = lax.Precision.HIGHEST


def product(left, right):
    return jnp.dot(left, right, precision=highest, preferred_element_type=jnp.float32)


def product_inner(left, right):
    return lax.dot_general(
        left, right, (((0,), (0,)), ((), ())), precision=highest, preferred_element_type=jnp.float32
    )


def solve_rows(gram, factor):
    lower = jnp.linalg.cholesky(gram)
    return jax.scipy.linalg.solve_triangular(lower, factor.T, lower=True).T


def orthonormal(factor):
    return solve_rows(product_inner(factor, factor), factor)


def orthonormal_rows(factor):
    gram = lax.psum(product_inner(factor, factor), "tensor")
    return solve_rows(gram, factor)


def local(
    grad_query,
    error_query,
    grad_output,
    error_output,
    start_query,
    start_output,
    weight_query,
    weight_output,
    moment_query,
    moment_output,
    grad_vector,
    moment_vector,
    weight_vector,
):
    replicas = lax.axis_size("shard")
    shard_index = lax.axis_index("shard")
    total_query = grad_query[0].astype(jnp.float32) + error_query[0]
    total_output = grad_output[0].astype(jnp.float32) + error_output[0]
    factor_query = start_query
    factor_output = start_output
    for turn in range(ROUNDS):
        part_query = product(total_query, factor_query)
        part_output = product(total_output, factor_output)
        sum_query = lax.psum(part_query, ("shard", "tensor"))
        sum_output = lax.psum(part_output, "shard")
        left_query = orthonormal(sum_query)
        left_output = orthonormal_rows(sum_output)
        right_query_part = product_inner(total_query, left_query)
        right_output_part = product_inner(total_output, left_output)
        factor_query = lax.psum(right_query_part, "shard")
        factor_output = lax.psum(right_output_part, ("shard", "tensor"))
    approx_query = product(left_query, factor_query.T) / replicas
    approx_output = product(left_output, factor_output.T) / replicas
    new_error_query = (total_query - approx_query)[None]
    new_error_output = (total_output - approx_output)[None]
    rows_block = moment_query.shape[0]
    block_query = lax.dynamic_slice_in_dim(approx_query, shard_index * rows_block, rows_block, 0)
    cols_block = moment_output.shape[1]
    block_output = lax.dynamic_slice_in_dim(approx_output, shard_index * cols_block, cols_block, 1)
    new_moment_query = 0.9 * moment_query + block_query
    new_moment_output = 0.9 * moment_output + block_output
    stepped_query = weight_query - 0.01 * new_moment_query
    stepped_output = weight_output - 0.01 * new_moment_output
    local_vector = grad_vector[0].astype(jnp.float32)
    vector_block = moment_vector.shape[0]
    vector_whole = lax.psum(local_vector, "shard")
    vector_part = lax.dynamic_slice_in_dim(
        vector_whole, shard_index * vector_block, vector_block, 0
    )
    vector_mean = vector_part / replicas
    new_moment_vector = 0.9 * moment_vector + vector_mean
    stepped_vector = weight_vector - 0.01 * new_moment_vector
    new_weight_query, new_weight_output, new_weight_vector = (
        lax.all_gather(stepped_query, "shard", axis=0, tiled=True),
        lax.all_gather(stepped_output, "shard", axis=1, tiled=True),
        lax.all_gather(stepped_vector, "shard", axis=0, tiled=True),
    )
    return (
        new_error_query,
        new_error_output,
        new_moment_query,
        new_moment_output,
        new_weight_query,
        new_weight_output,
        new_moment_vector,
        new_weight_vector,
    )


def solution(mesh):
    in_specs = (
        P("shard", None, "tensor"),
        P("shard", None, "tensor"),
        P("shard", "tensor", None),
        P("shard", "tensor", None),
        P("tensor", None),
        P(),
        P("shard", "tensor"),
        P("tensor", "shard"),
        P("shard", "tensor"),
        P("tensor", "shard"),
        P("shard", None),
        P("shard"),
        P("shard"),
    )
    out_specs = (
        P("shard", None, "tensor"),
        P("shard", "tensor", None),
        P("shard", "tensor"),
        P("tensor", "shard"),
        P(None, "tensor"),
        P("tensor", None),
        P("shard"),
        P(),
    )
    return jax.shard_map(local, mesh=mesh, in_specs=in_specs, out_specs=out_specs, check_vma=False)
```

profile of v0, /device:TPU:1, one launch (start us, length us, event | category | flops | bytes accessed | tf_op | source)
XLA Modules:
  0.0 2203.4 jit_solution(7634404734054702130)
XLA Ops:
  7.2 1.2 copy.45
  8.6 0.4 fusion.6
  9.1 498.1 %psum.81 = f32[128,32]{0,1:T(8,128)S(1)} all-reduce(f32[128,32]{0,1:T(8,128)S(1)} %fusion.6), channel_id=1, replica_groups=mesh['shard'=128,'tensor'=4] {'shard'}, use_global_device_ids=true, to_apply=%region_6.9 | all-reduce | flops 4096 | bytes 32768 | tf_op jit(solution)/shard_map/psum | solution.py:59
  507.3 13.2 psum.82
  520.6 2.9 cholesky.96
  523.6 0.6 compare_reduce_fusion.1
  524.2 0.7 fusion.24
  524.9 2.4 custom-call.12
  527.6 1.3 fusion.4
  528.9 1.3 fusion.15
  530.3 1.3 dynamic-slice
  532.3 265.7 %all-reduce.10.cloned.1.call-done = (f32[1024,32]{0,1:T(8,128)}, f32[1024,32]{0,1:T(8,128)}) async-done(((f32[1024,32]{0,1:T(8,128)}, f32[1024,32]{0,1:T(8,128)}), (f32[1024,32]{0,1:T(8,128)}, f32[1024,32]{0,1:T(8,128)})) %all-reduce.10.cloned.1.call-update) | async-done | bytes 262160 | tf_op jit(solution)/shard_map/psum | solution.py:58
  798.0 1.4 fusion.2
  799.7 2.9 cholesky.74
  802.7 0.6 compare_reduce_fusion.3
  803.3 0.7 fusion.22
  804.0 2.4 custom-call.10
  806.4 0.3 fusion.20
  806.8 0.4 fusion.13
  807.2 487.8 %all-reduce.4 = (f32[128,32]{0,1:T(8,128)S(1)}, f32[128,32]{0,1:T(8,128)S(1)}, f32[3584]{0:T(1024)S(1)}) all-reduce(f32[128,32]{0,1:T(8,128)S(1)} %fusion.13, f32[128,32]{0,1:T(8,128)S(1)} %fusion.2, f32[3584]{0:T(1024)S(1)} %convert_reduce_fusion), channel_id=1, replica_groups=mesh['shard'=128,'tensor'=4] {'shard'}, use_global_device_ids=true, to_apply=%region_3.6 | all-reduce | flops 11776 | bytes 94208 | tf_op jit(solution)/shard_map/psum | solution.py:64
  1295.2 12.4 psum.85
  1307.6 2.9 cholesky.107
  1310.6 0.6 compare_reduce_fusion
  1311.2 0.7 fusion.25
  1311.9 2.4 custom-call.13
  1314.6 1.3 fusion.11
  1315.9 1.3 fusion
  1317.3 0.6 copy-done.13
  1317.9 0.6 subtract_dynamic-update-slice_fusion
  1318.5 270.5 %all-reduce.8.cloned.1.call-done = (f32[1024,32]{0,1:T(8,128)}, f32[1024,32]{0,1:T(8,128)}) async-done(((f32[1024,32]{0,1:T(8,128)}, f32[1024,32]{0,1:T(8,128)}), (f32[1024,32]{0,1:T(8,128)}, f32[1024,32]{0,1:T(8,128)})) %all-reduce.8.cloned.1.call-update) | async-done | bytes 262160 | tf_op jit(solution)/shard_map/psum | solution.py:58
  1589.0 1.2 fusion.41
  1590.3 2.9 cholesky.85
  1593.3 0.6 compare_reduce_fusion.2
  1593.9 0.7 fusion.23
  1594.6 2.4 custom-call.11
  1597.0 0.3 fusion.18
  1597.4 0.4 fusion.9
  1597.8 487.8 %all-reduce.3 = (f32[128,32]{0,1:T(8,128)S(1)}, f32[3584]{0:T(1024)}) all-reduce(f32[128,32]{0,1:T(8,128)S(1)} %fusion.9, f32[3584]{0:T(1024)S(1)} %get-tuple-element.48), channel_id=1, replica_groups=mesh['shard'=128,'tensor'=4] {'shard'}, use_global_device_ids=true, to_apply=%region_5.8 | all-reduce | flops 7680 | bytes 61440 | tf_op jit(solution)/shard_map/psum | solution.py:64
  2085.6 1.0 convolution_multiply_fusion.1
  2086.6 0.9 fusion.17
  2087.5 1.0 convolution_multiply_fusion
  2088.6 1.0 copy.52
  2089.6 0.6 multiply_subtract_fusion
  2090.2 53.0 %all_gather.10 = f32[128,1024]{0,1:T(8,128)S(1)} all-gather(f32[128,8]{0,1:T(8,128)S(1)} %get-tuple-element.44), channel_id=1, replica_groups=mesh['shard'=128,'tensor'=4] {'shard'}, dimensions={1}, use_global_device_ids=true | all-gather | bytes 528384 | tf_op jit(solution)/shard_map/all_gather | solution.py:89
  2143.3 1.0 copy.53
  2144.3 0.6 multiply_subtract_fusion.1
  2144.9 50.9 %all_gather.9 = f32[1024,128]{1,0:T(8,128)S(1)} all-gather(f32[8,128]{1,0:T(8,128)S(1)} %get-tuple-element.46), channel_id=1, replica_groups=mesh['shard'=128,'tensor'=4] {'shard'}, dimensions={0}, use_global_device_ids=true | all-gather | bytes 528384 | tf_op jit(solution)/shard_map/all_gather | solution.py:88
  2195.8 0.8 copy.63
  (54 shorter events, 2.0 us)
Async XLA Ops:
  7.2 1.5 copy-start
  7.2 1.2 copy-start.5
  7.2 790.8 %all-reduce.10.cloned.1.call-start = ((), (), s32[]{:S(2)}) async-start(), calls=%async_computation.1 | async-start | bytes 524288 | tf_op jit(solution)/shard_map/psum | solution.py:58
  520.6 8.3 copy-start.1
  527.6 1.3 copy-start.2
  527.6 1.3 copy-start.7
  530.3 1058.7 %all-reduce.8.cloned.1.call-start = ((), (), s32[]{:S(2)}) async-start(), calls=%async_computation | async-start | bytes 524288 | tf_op jit(solution)/shard_map/psum | solution.py:58
  530.3 1.9 copy-start.8
  798.0 1.4 copy-start.3
  1317.2 0.7 copy-start.13
  1317.2 0.7 copy-start.14
  1590.2 6.8 copy-start.4
  2086.6 0.9 copy-start.6
  2088.6 1.0 copy-start.9
  2088.6 1.0 copy-start.10
  2143.3 1.0 copy-start.11
  2143.3 1.0 copy-start.12
Sparse Core Ops, SparseCore 0:
  530.4 267.5 all-reduce.9
  1317.3 271.6 all-reduce.7
where the time goes:
time: 2200 us
  blocking collectives  1600 us (73%)
  waiting for transfers between devices  536 us (24%)
  other arithmetic  29.5 us (1%)
    psum x2, blocking collectives, local(): factor_query = lax.psum(right_query_part, 'shard')  976 us
    psum x2, waiting for transfers between devices, local(): sum_query = lax.psum(part_query, ('shard', 'tensor'))  536 us
    psum x1, blocking collectives, local(): sum_output = lax.psum(part_output, 'shard')  498 us
    all_gather x1, blocking collectives, local(): lax.all_gather(stepped_output, 'shard', axis=1, tiled=True)  53 us
    all_gather x1, blocking collectives, local(): lax.all_gather(stepped_query, 'shard', axis=0, tiled=True)  50.9 us
  transfers between devices with their start and end apart: 2, of which 2 were waited for; matrix products, arithmetic and copies ran while one was open for 0% of the time, Pallas kernels for 0%

commit v1 on v0

--- a/solution.py
+++ b/solution.py
@@ -85,7 +85,10 @@
     new_moment_vector = 0.9 * moment_vector + vector_mean
     stepped_vector = weight_vector - 0.01 * new_moment_vector
     new_weight_query, new_weight_output, new_weight_vector = (
-        lax.all_gather(stepped_query, "shard", axis=0, tiled=True),
+        jnp.concatenate(
+            lax.all_to_all(jnp.stack([stepped_query] * lax.axis_size("shard")), "shard", 0, 0),
+            axis=0,
+        ),
         lax.all_gather(stepped_output, "shard", axis=1, tiled=True),
         lax.all_gather(stepped_vector, "shard", axis=0, tiled=True),
     )

time: 2200 us -> 2170 us (0.986)
  blocking collectives: 1600 us -> 1550 us
    all_gather x1 -> x0, blocking collectives: 50.9 us -> none  [local(): lax.all_gather(stepped_query, 'shard', axis=0, tiled=True)]
  transfers between devices with their start and end apart: 2 -> 3, of which waited for: 2 -> 2; matrix products, arithmetic and copies ran while one was open for 0% -> 0% of each run, Pallas kernels for 0% -> 0%
where the time goes in v1:
time: 2170 us
  blocking collectives  1550 us (71%)
  waiting for transfers between devices  536 us (25%)
  other arithmetic  29.5 us (1%)
    psum x2, blocking collectives, local(): factor_query = lax.psum(right_query_part, 'shard')  976 us
    psum x2, waiting for transfers between devices, local(): sum_query = lax.psum(part_query, ('shard', 'tensor'))  536 us
    psum x1, blocking collectives, local(): sum_output = lax.psum(part_output, 'shard')  498 us
    all_gather x1, blocking collectives, local(): lax.all_gather(stepped_output, 'shard', axis=1, tiled=True)  54.8 us
  transfers between devices with their start and end apart: 3, of which 2 were waited for; matrix products, arithmetic and copies ran while one was open for 0% of the time, Pallas kernels for 0%

profile of v1, /device:TPU:1, one launch (start us, length us, event | category | flops | bytes accessed | tf_op | source)
XLA Modules:
  0.0 2171.5 jit_solution(1115001216945083325)
XLA Ops:
  7.2 1.3 copy.46
  8.7 0.4 fusion.6
  9.2 498.1 %psum.81 = f32[128,32]{0,1:T(8,128)S(1)} all-reduce(f32[128,32]{0,1:T(8,128)S(1)} %fusion.6), channel_id=1, replica_groups=mesh['shard'=128,'tensor'=4] {'shard'}, use_global_device_ids=true, to_apply=%region_6.9 | all-reduce | flops 4096 | bytes 32768 | tf_op jit(solution)/shard_map/psum | solution.py:59
  507.4 13.2 psum.82
  520.7 2.9 cholesky.96
  523.7 0.6 compare_reduce_fusion.1
  524.3 0.7 fusion.24
  525.0 2.4 custom-call.12
  527.7 1.3 fusion.4
  529.0 1.3 fusion.15
  530.4 1.3 dynamic-slice
  532.4 265.7 %all-reduce.10.cloned.1.call-done = (f32[1024,32]{0,1:T(8,128)}, f32[1024,32]{0,1:T(8,128)}) async-done(((f32[1024,32]{0,1:T(8,128)}, f32[1024,32]{0,1:T(8,128)}), (f32[1024,32]{0,1:T(8,128)}, f32[1024,32]{0,1:T(8,128)})) %all-reduce.10.cloned.1.call-update) | async-done | bytes 262160 | tf_op jit(solution)/shard_map/psum | solution.py:58
  798.1 1.2 fusion.40
  799.4 2.9 cholesky.74
  802.4 0.6 compare_reduce_fusion.3
  803.0 0.7 fusion.22
  803.7 2.4 custom-call.10
  806.5 0.4 fusion.13
  806.9 0.4 copy-done.6
  807.4 0.4 fusion.2
  807.8 487.8 %all-reduce.4 = (f32[128,32]{0,1:T(8,128)S(1)}, f32[128,32]{0,1:T(8,128)S(1)}, f32[3584]{0:T(1024)S(1)}) all-reduce(f32[128,32]{0,1:T(8,128)S(1)} %fusion.13, f32[128,32]{0,1:T(8,128)S(1)} %fusion.2, f32[3584]{0:T(1024)S(1)} %convert_reduce_fusion), channel_id=1, replica_groups=mesh['shard'=128,'tensor'=4] {'shard'}, use_global_device_ids=true, to_apply=%region_3.6 | all-reduce | flops 11776 | bytes 94208 | tf_op jit(solution)/shard_map/psum | solution.py:64
  1295.6 1.3 fusion.11
  1297.1 12.3 psum.85
  1309.4 2.9 cholesky.107
  1312.4 0.6 compare_reduce_fusion
  1313.0 0.7 fusion.25
  1313.7 2.4 custom-call.13
  1316.4 1.3 fusion
  1317.7 0.6 copy-done.14
  1318.4 0.6 subtract_dynamic-update-slice_fusion
  1319.0 270.6 %all-reduce.8.cloned.1.call-done = (f32[1024,32]{0,1:T(8,128)}, f32[1024,32]{0,1:T(8,128)}) async-done(((f32[1024,32]{0,1:T(8,128)}, f32[1024,32]{0,1:T(8,128)}), (f32[1024,32]{0,1:T(8,128)}, f32[1024,32]{0,1:T(8,128)})) %all-reduce.8.cloned.1.call-update) | async-done | bytes 262160 | tf_op jit(solution)/shard_map/psum | solution.py:58
  1589.6 1.2 fusion.41
  1590.9 2.9 cholesky.85
  1593.8 0.6 compare_reduce_fusion.2
  1594.5 0.7 fusion.23
  1595.1 2.4 custom-call.11
  1598.4 487.8 %all-reduce.3 = (f32[128,32]{0,1:T(8,128)S(1)}, f32[3584]{0:T(1024)}) all-reduce(f32[128,32]{0,1:T(8,128)S(1)} %fusion.9, f32[3584]{0:T(1024)S(1)} %get-tuple-element.48), channel_id=1, replica_groups=mesh['shard'=128,'tensor'=4] {'shard'}, use_global_device_ids=true, to_apply=%region_5.8 | all-reduce | flops 7680 | bytes 61440 | tf_op jit(solution)/shard_map/psum | solution.py:64
  2086.2 1.0 convolution_multiply_fusion.1
  2087.2 0.6 multiply_subtract_fusion.1
  2087.8 0.8 stack.2
  2088.6 14.8 all-to-all-start
  2103.4 1.0 convolution_multiply_fusion
  2104.5 1.0 copy.52
  2105.5 0.6 multiply_subtract_fusion
  2106.1 54.8 %all_gather.6 = f32[128,1024]{0,1:T(8,128)S(1)} all-gather(f32[128,8]{0,1:T(8,128)S(1)} %get-tuple-element.44), channel_id=1, replica_groups=mesh['shard'=128,'tensor'=4] {'shard'}, dimensions={1}, use_global_device_ids=true | all-gather | bytes 528384 | tf_op jit(solution)/shard_map/all_gather | solution.py:92
  2161.0 1.0 copy.53
  2162.0 0.9 fusion.17
  2162.8 1.9 copy.63
  (58 shorter events, 2.8 us)
Async XLA Ops:
  7.2 1.6 copy-start
  7.2 1.4 copy-start.5
  7.2 790.9 %all-reduce.10.cloned.1.call-start = ((), (), s32[]{:S(2)}) async-start(), calls=%async_computation.2 | async-start | bytes 524288 | tf_op jit(solution)/shard_map/psum | solution.py:58
  520.7 8.3 copy-start.1
  527.7 1.3 copy-start.2
  527.7 1.3 copy-start.8
  530.3 1059.2 %all-reduce.8.cloned.1.call-start = ((), (), s32[]{:S(2)}) async-start(), calls=%async_computation.1 | async-start | bytes 524288 | tf_op jit(solution)/shard_map/psum | solution.py:58
  530.4 1.9 copy-start.9
  799.3 6.8 copy-start.3
  806.5 0.9 copy-start.6
  1317.7 0.7 copy-start.14
  1317.7 0.7 copy-start.15
  1590.8 6.8 copy-start.4
  2086.2 1.0 copy-start.10
  2086.2 1.0 copy-start.11
  2088.6 14.8 copy-start.7
  2088.6 74.2 %all-to-all-start = ((f32[128,8,128]{2,1,0:T(8,128)}), f32[128,8,128]{2,1,0:T(8,128)}, u32[]{:S(2)}, u32[]{:S(2)}) async-start(f32[128,8,128]{2,1,0:T(8,128)} %stack.2), calls=%async_computation | async-start | bytes 1048576 | tf_op jit(solution)/shard_map/all_to_all | solution.py:89
  2104.5 1.0 copy-start.12
  2104.5 1.0 copy-start.13
Sparse Core Ops, SparseCore 0:
  530.5 267.5 all-reduce.9
  1317.8 271.6 all-reduce.7
